TPU v7x, 32 devices: a whole 2x2x4 slice. The times are simulated.
32 devices in a mesh: dp: 8 (over y, x, core), ctx: 4 (over z).
Axes of the slice: x: 2, y: 2, z: 4, core: 2. Of those that a mesh axis runs over, the one named last changes fastest.
Arguments:
- query_proj: bfloat16 [8, 512, 4096], P('dp', 'ctx'), may hold values from -6 to 6
- key_proj: bfloat16 [8, 512, 4096], P('dp', 'ctx'), may hold values from -6 to 6
- value_proj: bfloat16 [8, 512, 4096], P('dp', 'ctx'), may hold values from -6 to 6
- offsets: int32 [8, 512], P('dp', 'ctx'), may hold values from 0 to 511, as said below
- filter_taps: float32 [256, 128], P(('dp', 'ctx')), may hold values from -1.2 to 1.2
- filter_decay: float32 [256], P(('dp', 'ctx')), may hold values from 0.003125 to 0.09375
- out_weight: bfloat16 [4096, 8192], P('dp', 'ctx'), may hold values from -0.09375 to 0.09375
- grad_mixed: bfloat16 [8, 512, 8192], P('dp', None, 'ctx'), may hold values from -1.5 to 1.5
Outputs:
- mixed: bfloat16 [8, 512, 8192], P('dp', None, 'ctx')
- grad_query: bfloat16 [8, 512, 4096], P('dp', 'ctx')
- grad_key: bfloat16 [8, 512, 4096], P('dp', 'ctx')
- grad_value: bfloat16 [8, 512, 4096], P('dp', 'ctx')
- grad_weight: float32 [4096, 8192], P('dp', 'ctx')
- grad_taps: float32 [256, 128], P(('dp', 'ctx'))
- grad_decay: float32 [256], P(('dp', 'ctx'))
Inputs may be any that keep to these rules, and one draw needn't show every extreme that they name: offsets is 0 at the first base of every window and of every contig, and otherwise one more than at the base before.
All inputs are finite; a program needn't handle non-finite values.
Results may differ from a plain program's by a relative error of at most 0.02.
Values may be sent and summed in bfloat16 or wider, within the bound.
A program may use at most 192 MiB of HBM per device.

v0:
```python
import jax
import jax.numpy as jnp
from jax import lax
from jax.sharding import PartitionSpec as P


def shifted(value, axis, by):
    length = lax.axis_size(axis)
    pairs = [(i, i + by) for i in range(length) if 0 <= i + by < length]
    return lax.ppermute(value, axis, pairs)


def build_toeplitz(filter_bf, offset_loc, row_count, span_rows):
    tap_count = filter_bf.shape[1]
    group_count = filter_bf.shape[0]
    reversed_taps = filter_bf.T[::-1]
    base_rows = jnp.concatenate(
        [reversed_taps, jnp.zeros((span_rows + 1 - tap_count, group_count), jnp.bfloat16)], axis=0
    )
    tiled = jnp.tile(base_rows, (row_count, 1))[: row_count * span_rows]
    tiled = tiled.reshape(row_count, span_rows, group_count)
    out_rows = jnp.arange(row_count, dtype=jnp.int32)[:, None]
    in_rows = jnp.arange(span_rows, dtype=jnp.int32)[None, :]
    lag_index = out_rows + tap_count - 1 - in_rows
    allowed = lag_index <= offset_loc[:, None]
    return jnp.where(allowed[:, :, None], tiled, jnp.zeros((), jnp.bfloat16))


def local(
    query_proj, key_proj, value_proj, offsets, filter_taps, filter_decay, out_weight, grad_mixed
):
    query_loc = query_proj[0]
    key_loc = key_proj[0]
    value_loc = value_proj[0]
    offset_loc = offsets[0]
    cotangent = grad_mixed[0]
    row_count = query_loc.shape[0]
    chan_count = query_loc.shape[1]
    tap_count = filter_taps.shape[1]
    reach_rows = tap_count - 1
    span_rows = row_count + reach_rows
    taps_all, decay_all = (
        lax.all_gather(filter_taps, ("dp", "ctx"), axis=0, tiled=True),
        lax.all_gather(filter_decay, ("dp", "ctx"), axis=0, tiled=True),
    )
    group_count = taps_all.shape[0]
    group_width = chan_count // group_count
    tap_index = jnp.arange(tap_count, dtype=jnp.float32)
    decay_env = jnp.exp(-decay_all[:, None] * tap_index[None, :])
    filter_bf = (taps_all * decay_env).astype(jnp.bfloat16)
    mixer_in = (key_loc.astype(jnp.float32) * value_loc.astype(jnp.float32)).astype(jnp.bfloat16)
    previous = shifted(mixer_in[row_count - reach_rows :], "ctx", 1)
    mixer_ext = jnp.concatenate([previous, mixer_in], axis=0)
    toeplitz = build_toeplitz(filter_bf, offset_loc, row_count, span_rows)
    mixer3 = mixer_ext.reshape(span_rows, group_count, group_width)
    conv_out = jnp.einsum(
        "tsg,sgc->tgc", toeplitz, mixer3, preferred_element_type=jnp.float32
    ).reshape(row_count, chan_count)
    gated = (query_loc.astype(jnp.float32) * conv_out).astype(jnp.bfloat16)
    weight_full = lax.all_gather(out_weight, "dp", axis=0, tiled=True)
    gated_full = lax.all_gather(gated, "ctx", axis=0, tiled=True)
    mixed = jnp.dot(gated_full, weight_full, preferred_element_type=jnp.float32).astype(
        jnp.bfloat16
    )
    grad_gated = lax.psum_scatter(
        lax.dot_general(
            cotangent, weight_full, (((1,), (1,)), ((), ())), preferred_element_type=jnp.float32
        ).astype(jnp.bfloat16),
        "ctx",
        scatter_dimension=0,
        tiled=True,
    ).astype(jnp.float32)
    grad_query = (grad_gated * conv_out).astype(jnp.bfloat16)
    grad_conv = (grad_gated * query_loc.astype(jnp.float32)).astype(jnp.bfloat16)
    grad3 = grad_conv.reshape(row_count, group_count, group_width)
    grad_ext = jnp.einsum(
        "tsg,tgc->sgc", toeplitz, grad3, preferred_element_type=jnp.float32
    ).reshape(span_rows, chan_count)
    spill = shifted(grad_ext[:reach_rows].astype(jnp.bfloat16), "ctx", -1).astype(jnp.float32)
    grad_mixer = grad_ext[reach_rows:].at[row_count - reach_rows :].add(spill)
    grad_key = (grad_mixer * value_loc.astype(jnp.float32)).astype(jnp.bfloat16)
    grad_value = (grad_mixer * key_loc.astype(jnp.float32)).astype(jnp.bfloat16)
    block_count = 4
    block_size = group_count // block_count
    lag_keep = (reach_rows - jnp.arange(tap_count, dtype=jnp.int32))[None, :] <= offset_loc[:, None]
    pieces = []
    for block_index in range(block_count):
        low_group = block_index * block_size
        products = jnp.einsum(
            "tgc,sgc->tsg",
            grad3[:, low_group : low_group + block_size],
            mixer3[:, low_group : low_group + block_size],
            preferred_element_type=jnp.float32,
        )
        flattened = products.reshape(row_count * span_rows, block_size)
        flattened = jnp.concatenate(
            [flattened, jnp.zeros((row_count, block_size), jnp.float32)], axis=0
        )
        diagonal = flattened.reshape(row_count, span_rows + 1, block_size)[:, :tap_count]
        pieces.append(jnp.sum(jnp.where(lag_keep[:, :, None], diagonal, jnp.float32(0.0)), axis=0))
    by_lag = jnp.concatenate(pieces, axis=1)
    grad_filter = by_lag[::-1].T
    taps_part = grad_filter * decay_env
    decay_part = -jnp.sum(tap_index[None, :] * grad_filter * taps_all * decay_env, axis=1)
    grad_taps, grad_decay = (
        lax.psum_scatter(taps_part, ("dp", "ctx"), scatter_dimension=0, tiled=True),
        lax.psum_scatter(decay_part, ("dp", "ctx"), scatter_dimension=0, tiled=True),
    )
    grad_weight = lax.psum_scatter(
        lax.dot_general(
            gated_full, cotangent, (((0,), (0,)), ((), ())), preferred_element_type=jnp.float32
        ).astype(jnp.bfloat16),
        "dp",
        scatter_dimension=0,
        tiled=True,
    ).astype(jnp.float32)
    return (
        mixed[None],
        grad_query[None],
        grad_key[None],
        grad_value[None],
        grad_weight,
        grad_taps,
        grad_decay,
    )


def solution(mesh):
    in_specs = (
        P("dp", "ctx", None),
        P("dp", "ctx", None),
        P("dp", "ctx", None),
        P("dp", "ctx"),
        P(("dp", "ctx"), None),
        P(("dp", "ctx")),
        P("dp", "ctx"),
        P("dp", None, "ctx"),
    )
    out_specs = (
        P("dp", None, "ctx"),
        P("dp", "ctx", None),
        P("dp", "ctx", None),
        P("dp", "ctx", None),
        P("dp", "ctx"),
        P(("dp", "ctx"), None),
        P(("dp", "ctx")),
    )
    return jax.shard_map(local, mesh=mesh, in_specs=in_specs, out_specs=out_specs, check_vma=False)
```

profile of v0, /device:TPU:0, one launch (start us, length us, event | category | flops | bytes accessed | tf_op | source)
XLA Modules:
  0.0 786.9 jit_solution(17749648390196525107)
XLA Ops:
  8.0 94.5 %all-gather.5.cloned.1.call-done = bf16[4096,2048]{1,0:T(8,128)(2,1)} async-done(((bf16[512,2048]{1,0:T(8,128)(2,1)}), bf16[4096,2048]{1,0:T(8,128)(2,1)}) %all-gather.5.cloned.1.call-update) | async-done | bytes 16777232 | tf_op jit(solution)/shard_map/all_gather | solution.py:60
  102.5 13.8 %convolution_convert_fusion.1 = bf16[512,4096]{1,0:T(8,128)(2,1)} fusion(bf16[4096,2048]{1,0:T(8,128)(2,1)} %all-gather.5.cloned.1.call-done, bf16[1,512,2048]{2,1,0:T(8,128)(2,1)S(1)} %copy-done), kind=kOutput, calls=%fused_computation.2 | convolution fusion | flops 8592031744 | bytes 23068672 | tf_op jit(solution)/shard_map/dot_general | solution.py:66
  117.1 41.7 %all-reduce.5 = f32[256]{0:T(256)S(1)} all-reduce(f32[256]{0:T(256)S(1)} %dynamic-update-slice.3), channel_id=1, replica_groups=mesh['dp'=8,'ctx'=4] {'dp','ctx'}, use_global_device_ids=true, to_apply=%add.5 | all-reduce | flops 256 | bytes 2048
  158.8 71.1 %all_gather.12 = f32[256,128]{1,0:T(8,128)S(1)} all-gather(f32[8,128]{1,0:T(8,128)S(1)} %copy-done.11), channel_id=1, replica_groups=mesh['dp'=8,'ctx'=4] {'dp','ctx'}, dimensions={0}, use_global_device_ids=true | all-gather | bytes 135168 | tf_op jit(solution)/shard_map/all_gather | solution.py:43
  233.1 6.5 slice.93
  239.6 19.0 %reshape.175 = bf16[128,255,256]{2,1,0:T(8,128)(2,1)} reshape(bf16[32640,256]{1,0:T(8,128)(2,1)} %slice.93) | data formatting | bytes 33423360 | tf_op jit(solution)/shard_map/reshape | solution.py:21
  258.8 11.9 %broadcast_select_fusion = bf16[128,255,256]{2,1,0:T(8,128)(2,1)} fusion(bf16[128,255,256]{2,1,0:T(8,128)(2,1)} %reshape.175, pred[128,255]{1,0:T(8,128)(4,1)S(1)} %subtract_compare_fusion), kind=kLoop, calls=%fused_computation | loop fusion | flops 8355840 | bytes 33456000 | tf_op jit(solution)/shard_map/jit(_where)/select_n | solution.py:26
  270.7 23.3 %copy.42 = bf16[128,255,256]{1,0,2:T(8,128)(2,1)} copy(bf16[128,255,256]{2,1,0:T(8,128)(2,1)} %broadcast_select_fusion) | data formatting | bytes 33423360 | tf_op jit(solution)/shard_map/jit(_where)/select_n | solution.py:26
  298.1 7.0 convolution_bitcast_fusion.4
  312.2 4.1 slice.94
  317.9 2.9 copy.49
  320.8 2.9 copy.48
  323.7 9.6 %collective-permute-done.1 = bf16[127,4096]{1,0:T(8,128)(2,1)} collective-permute-done((bf16[127,4096]{1,0:T(8,128)(2,1)}, bf16[127,4096]{1,0:T(8,128)(2,1)}, u32[]{:S(2)}, u32[]{:S(2)}) %collective-permute-start.1) | collective-permute-done | bytes 1040416 | tf_op jit(solution)/shard_map/ppermute | solution.py:10
  333.4 3.4 convert_add_fusion
  336.8 6.3 scatter-add.4
  343.1 4.2 fusion.13
  349.9 16.0 %collective-permute-done = bf16[127,4096]{1,0:T(8,128)(2,1)S(1)} collective-permute-done((bf16[127,4096]{1,0:T(8,128)(2,1)S(1)}, bf16[127,4096]{1,0:T(8,128)(2,1)S(1)}, u32[]{:S(2)}, u32[]{:S(2)}) %collective-permute-start) | collective-permute-done | bytes 1040416 | tf_op jit(solution)/shard_map/ppermute | solution.py:10
  367.6 4.1 copy.40
  371.6 12.2 %fusion.24 = f32[256,16,128]{2,1,0:T(8,128)} fusion(bf16[255,256,16]{0,2,1:T(8,128)(2,1)} %bitcast.103, bf16[128,255,256]{1,0,2:T(8,128)(2,1)} %copy.42), kind=kOutput, calls=%fused_computation.56 | convolution fusion | flops 267386880 | bytes 20897792 | tf_op jit(solution)/shard_map/tsg,sgc->tgc/dot_general | solution.py:56
  383.8 5.7 convolution_bitcast_fusion.3
  389.5 4.5 convolution_bitcast_fusion.2
  394.0 4.5 convolution_bitcast_fusion.1
  398.5 2.9 copy.43
  401.4 4.0 fusion.15
  405.7 9.0 %copy.50 = f32[128,255,64]{1,0,2:T(8,128)} copy(f32[128,255,64]{0,1,2:T(8,128)} %convolution_bitcast_fusion.3) | data formatting | bytes 16711680 | tf_op jit(solution)/shard_map/tgc,sgc->tsg/transpose | solution.py:89
  414.7 9.6 %reshape.179 = f32[32640,64]{0,1:T(8,128)} reshape(f32[128,255,64]{1,0,2:T(8,128)} %copy.50) | data formatting | bytes 16711680 | tf_op jit(solution)/shard_map/reshape | solution.py:95
  424.4 4.1 concatenate.25
  428.5 5.7 copy.55
  434.2 9.0 %copy.51 = f32[128,255,64]{1,0,2:T(8,128)} copy(f32[128,255,64]{0,1,2:T(8,128)} %convolution_bitcast_fusion.2) | data formatting | bytes 16711680 | tf_op jit(solution)/shard_map/tgc,sgc->tsg/transpose | solution.py:89
  443.2 9.3 %reshape.181 = f32[32640,64]{0,1:T(8,128)} reshape(f32[128,255,64]{1,0,2:T(8,128)} %copy.51) | data formatting | bytes 16711680 | tf_op jit(solution)/shard_map/reshape | solution.py:95
  452.5 4.1 concatenate.26
  456.6 5.7 copy.56
  462.3 9.0 %copy.52 = f32[128,255,64]{1,0,2:T(8,128)} copy(f32[128,255,64]{0,1,2:T(8,128)} %convolution_bitcast_fusion.1) | data formatting | bytes 16711680 | tf_op jit(solution)/shard_map/tgc,sgc->tsg/transpose | solution.py:89
  471.3 9.6 %reshape.183 = f32[32640,64]{0,1:T(8,128)} reshape(f32[128,255,64]{1,0,2:T(8,128)} %copy.52) | data formatting | bytes 16711680 | tf_op jit(solution)/shard_map/reshape | solution.py:95
  480.9 4.0 concatenate.27
  485.0 5.7 copy.57
  490.7 4.5 convolution_bitcast_fusion
  495.2 9.0 %copy.53 = f32[128,255,64]{1,0,2:T(8,128)} copy(f32[128,255,64]{0,1,2:T(8,128)} %convolution_bitcast_fusion) | data formatting | bytes 16711680 | tf_op jit(solution)/shard_map/tgc,sgc->tsg/transpose | solution.py:89
  504.2 9.2 %reshape.185 = f32[32640,64]{0,1:T(8,128)} reshape(f32[128,255,64]{1,0,2:T(8,128)} %copy.53) | data formatting | bytes 16711680 | tf_op jit(solution)/shard_map/reshape | solution.py:95
  513.4 4.2 concatenate.28
  517.6 5.7 copy.58
  523.4 6.4 fusion.3
  530.9 14.8 %convolution_convert_fusion = bf16[4096,2048]{1,0:T(8,128)(2,1)} fusion(bf16[512,4096]{1,0:T(8,128)(2,1)} %all-gather.3.cloned.1.call-done, bf16[1,512,2048]{2,1,0:T(8,128)(2,1)S(1)} %copy-done), kind=kOutput, calls=%fused_computation.1 | convolution fusion | flops 8598323200 | bytes 23068672 | tf_op jit(solution)/shard_map/dot_general | solution.py:110
  545.8 44.5 %all-reduce.7 = f32[256]{0:T(256)S(1)} all-reduce(f32[256]{0:T(256)S(1)} %neg.8), channel_id=5, replica_groups=mesh['dp'=8,'ctx'=4] {'dp','ctx'}, use_global_device_ids=true, to_apply=%region_8.9.clone | all-reduce | flops 256 | bytes 2048
  590.9 66.3 %all-reduce.10.cloned.1.call-done = f32[256,128]{1,0:T(8,128)} async-done(((f32[256,128]{1,0:T(8,128)}), f32[256,128]{1,0:T(8,128)}) %all-reduce.10.cloned.1.call-update) | async-done | bytes 131088
  658.5 14.5 %fusion.4 = bf16[1,512,2048]{2,1,0:T(8,128)(2,1)} fusion(bf16[512,4096]{1,0:T(8,128)(2,1)} %all-gather.3.cloned.1.call-done, bf16[4096,2048]{1,0:T(8,128)(2,1)} %all-gather.5.cloned.1.call-done), kind=kOutput, calls=%fused_computation.16 | convolution fusion | flops 8590983168 | bytes 23068672 | tf_op jit(solution)/shard_map/dot_general | solution.py:62
  673.1 103.0 %reduce-scatter.5.cloned.1.call-done = bf16[512,2048]{1,0:T(8,128)(2,1)} async-done(((bf16[4096,2048]{1,0:T(8,128)(2,1)}), bf16[512,2048]{1,0:T(8,128)(2,1)}) %reduce-scatter.5.cloned.1.call-update) | async-done | bytes 2097168 | tf_op jit(solution)/shard_map/reduce_scatter | solution.py:109
  776.1 4.1 convert_element_type.83
  (72 shorter events, 25.2 us)
Async XLA Ops:
  7.2 95.3 %copy-start = (bf16[1,512,2048]{2,1,0:T(8,128)(2,1)S(1)}, bf16[1,512,2048]{2,1,0:T(8,128)(2,1)}, u32[]{:S(2)}) copy-start(bf16[1,512,2048]{2,1,0:T(8,128)(2,1)} %param.17) | copy-start | bytes 6291460
  7.2 95.3 %all-gather.5.cloned.1.call-start = ((), (), s32[]{:S(2)}) async-start(), calls=%async_computation.3 | async-start | bytes 18874368 | tf_op jit(solution)/shard_map/all_gather | solution.py:60
  7.9 286.1 %reduce-scatter.3.cloned.1.call-start = ((), (), s32[]{:S(2)}) async-start(), calls=%async_computation.4 | async-start | bytes 5242880 | tf_op jit(solution)/shard_map/reduce_scatter | solution.py:65
  116.3 0.7 copy-start.13
  116.3 42.5 %copy-start.11 = (f32[8,128]{1,0:T(8,128)S(1)}, f32[8,128]{1,0:T(8,128)}, u32[]{:S(2)}) copy-start(f32[8,128]{1,0:T(8,128)} %param.14) | copy-start | bytes 12292
  116.3 414.6 %all-gather.3.cloned.1.call-start = ((), (), s32[]{:S(2)}) async-start(), calls=%async_computation.2 | async-start | bytes 5242880 | tf_op jit(solution)/shard_map/all_gather | solution.py:61
  158.8 71.1 %copy-start.9 = (f32[256]{0:T(256)}, f32[256]{0:T(256)S(1)}, u32[]{:S(2)}) copy-start(f32[256]{0:T(256)S(1)} %neg.7) | copy-start | bytes 3076
  229.9 0.6 copy-start.6
  239.6 19.0 %copy-start.12 = (s32[1,128]{1,0:T(1,128)S(1)}, s32[1,128]{1,0:T(1,128)}, u32[]{:S(2)}) copy-start(s32[1,128]{1,0:T(1,128)} %param.13) | copy-start | bytes 1540
  270.7 23.3 %copy-start.5 = (bf16[1,128,4096]{2,1,0:T(8,128)(2,1)S(1)}, bf16[1,128,4096]{2,1,0:T(8,128)(2,1)}, u32[]{:S(2)}) copy-start(bf16[1,128,4096]{2,1,0:T(8,128)(2,1)} %param.10) | copy-start | bytes 3145732
  305.1 2.0 copy-start.1
  310.7 5.7 copy-start.2
  310.7 22.7 %collective-permute-start.1 = (bf16[127,4096]{1,0:T(8,128)(2,1)}, bf16[127,4096]{1,0:T(8,128)(2,1)}, u32[]{:S(2)}, u32[]{:S(2)}) collective-permute-start(bf16[127,4096]{1,0:T(8,128)(2,1)} %copy.47), channel_id=1, source_target_pairs={{1,0},{2,1},{3,2},{5,4},{6,5},{7,6},{9,8},{10,9},{11,10},{13,12},{... | collective-permute-start | bytes 3121160 | tf_op jit(solution)/shard_map/ppermute | solution.py:10
  347.5 18.4 %collective-permute-start = (bf16[127,4096]{1,0:T(8,128)(2,1)S(1)}, bf16[127,4096]{1,0:T(8,128)(2,1)S(1)}, u32[]{:S(2)}, u32[]{:S(2)}) collective-permute-start(bf16[127,4096]{1,0:T(8,128)(2,1)S(1)} %slice.92), channel_id=1, source_target_pairs={{0,1},{1,2},{2,3},{4,5},{5,6},{6,7},{8,9},{9,10},{10,11},{12,13},{... | collective-permute-start | bytes 3121160 | tf_op jit(solution)/shard_map/ppermute | solution.py:10
  383.8 5.7 copy-start.3
  405.5 251.7 %all-reduce.10.cloned.1.call-start = ((), (), s32[]{:S(2)}) async-start(), calls=%async_computation.6 | async-start | bytes 262144
  485.0 5.7 copy-start.4
  513.4 9.9 %slice-start = ((s8[8388608]{0:T(1024)(128)(4,1)}), s8[4194304]{0:T(1024)(128)(4,1)S(1)}, s32[]{:S(2)}) async-start(s8[8388608]{0:T(1024)(128)(4,1)} %bitcast.97), calls=%async_computation.7 | async-start | bytes 8388608
  517.6 5.7 slice-start.1
  517.6 5.7 copy-start.8
  523.4 6.7 copy-start.7
  523.4 6.7 copy-start.10
  530.9 245.2 %reduce-scatter.5.cloned.1.call-start = ((), (), s32[]{:S(2)}) async-start(), calls=%async_computation.5 | async-start | bytes 18874368 | tf_op jit(solution)/shard_map/reduce_scatter | solution.py:109
Sparse Core Ops, SparseCore 0:
  9.9 92.5 all-gather.4
  116.4 79.0 reduce-scatter.2
  405.6 84.6 all-gather.2
  531.0 126.1 all-reduce.9
  661.1 114.9 reduce-scatter.4
where the time goes:
time: 798 us; the launch traced here: 787 us
  waiting for transfers between devices  290 us (36%)
  local copies, waits for them, and re-layouts  200 us (25%)
  blocking collectives  157 us (20%)
  matrix products  81.5 us (10%)
  other arithmetic  39.9 us (5%)
  between operations  14.3 us (2%)
    reduce_scatter x1, waiting for transfers between devices, local(): lax.psum_scatter(lax.dot_general(gated_full, cotangent, (((0,), (0,)), ((...  103 us
    all_gather x1, waiting for transfers between devices, local(): weight_full = lax.all_gather(out_weight, 'dp', axis=0, tiled=True)  94.5 us
    unnamed x2, blocking collectives  86.2 us
    all_gather x1, blocking collectives, local(): lax.all_gather(filter_taps, ('dp', 'ctx'), axis=0, tiled=True)  71.1 us
    unnamed x6, waiting for transfers between devices  67.1 us
    reshape x4, local copies, waits for them, and re-layouts, local(): flattened = products.reshape(row_count * span_rows, block_size)  37.8 us
    transpose x4, local copies, waits for them, and re-layouts, local(): jnp.einsum('tgc,sgc->tsg', grad3[:, low_group:low_group + block_size], mi...  36 us
    unnamed x41, local copies, waits for them, and re-layouts  28.3 us
  transfers between devices with their start and end apart: 7, of which 5 were waited for; matrix products, arithmetic and copies ran while one was open for 29% of the time, Pallas kernels for 0%

commit v1 on v0

--- a/solution.py
+++ b/solution.py
@@ -2,6 +2,19 @@
 import jax.numpy as jnp
 from jax import lax
 from jax.sharding import PartitionSpec as P
+
+
+def ring_gather(x, axis, dim):
+    ways = lax.axis_size(axis)
+    up = [(d, (d + 1) % ways) for d in range(ways)]
+    down = [(d, (d - 1) % ways) for d in range(ways)]
+    earlier, later = ([x], [x])
+    for _ in range(ways // 2):
+        earlier.append(lax.ppermute(earlier[-1], axis, up))
+    for _ in range((ways - 1) // 2):
+        later.append(lax.ppermute(later[-1], axis, down))
+    line = jnp.concatenate([*earlier[::-1], *later[1:]], axis=dim)
+    return jnp.roll(line, (lax.axis_index(axis) - ways // 2) * x.shape[dim], axis=dim)
 
 
 def shifted(value, axis, by):
@@ -57,7 +70,7 @@
         "tsg,sgc->tgc", toeplitz, mixer3, preferred_element_type=jnp.float32
     ).reshape(row_count, chan_count)
     gated = (query_loc.astype(jnp.float32) * conv_out).astype(jnp.bfloat16)
-    weight_full = lax.all_gather(out_weight, "dp", axis=0, tiled=True)
+    weight_full = ring_gather(out_weight, "dp", 0)
     gated_full = lax.all_gather(gated, "ctx", axis=0, tiled=True)
     mixed = jnp.dot(gated_full, weight_full, preferred_element_type=jnp.float32).astype(
         jnp.bfloat16

time: 798 us -> 917 us (1.15)
  waiting for transfers between devices: 290 us -> 351 us
  local copies, waits for them, and re-layouts: 200 us -> 246 us
    ppermute x0 -> x7, waiting for transfers between devices: none -> 157 us  [the longest x4 156 us: ring_gather(): earlier.append(lax.ppermute(earlier[-1], axis, up))]
    all_gather x1 -> x0, waiting for transfers between devices: 94.5 us -> none  [local(): weight_full = lax.all_gather(out_weight, 'dp', axis=0, tiled=True)]
    unnamed x41 -> x88, local copies, waits for them, and re-layouts: 28.3 us -> 77.6 us
    unnamed x2, blocking collectives: 86.2 us -> 95.9 us
  transfers between devices with their start and end apart: 7 -> 13, of which waited for: 5 -> 9; matrix products, arithmetic and copies ran while one was open for 29% -> 28% of each run, Pallas kernels for 0% -> 0%
where the time goes in v1:
time: 917 us; the launch traced here: 907 us
  waiting for transfers between devices  351 us (38%)
  local copies, waits for them, and re-layouts  246 us (27%)
  blocking collectives  166 us (18%)
  matrix products  82.1 us (9%)
  other arithmetic  36.3 us (4%)
  between operations  14.3 us (2%)
  starting transfers between devices  12.2 us (1%)
    ppermute x4, waiting for transfers between devices, ring_gather(): earlier.append(lax.ppermute(earlier[-1], axis, up))  156 us
    reduce_scatter x1, waiting for transfers between devices, local(): lax.psum_scatter(lax.dot_general(gated_full, cotangent, (((0,), (0,)), ((...  103 us
    unnamed x2, blocking collectives  95.9 us
    unnamed x88, local copies, waits for them, and re-layouts  77.6 us
    all_gather x1, blocking collectives, local(): lax.all_gather(filter_taps, ('dp', 'ctx'), axis=0, tiled=True)  70 us
    unnamed x6, waiting for transfers between devices  64.3 us
    reshape x4, local copies, waits for them, and re-layouts, local(): flattened = products.reshape(row_count * span_rows, block_size)  37.8 us
    transpose x4, local copies, waits for them, and re-layouts, local(): jnp.einsum('tgc,sgc->tsg', grad3[:, low_group:low_group + block_size], mi...  35.9 us
  transfers between devices with their start and end apart: 13, of which 9 were waited for; matrix products, arithmetic and copies ran while one was open for 28% of the time, Pallas kernels for 0%

profile of v1, /device:TPU:0, one launch (start us, length us, event | category | flops | bytes accessed | tf_op | source)
XLA Modules:
  0.0 907.4 jit_solution(18004291090211620816)
XLA Ops:
  7.7 26.8 %collective-permute-done.1 = bf16[512,2048]{1,0:T(8,128)(2,1)S(1)} collective-permute-done((bf16[512,2048]{1,0:T(8,128)(2,1)}, bf16[512,2048]{1,0:T(8,128)(2,1)S(1)}, u32[]{:S(2)}, u32[]{:S(2)}) %collective-permute-start.1) | collective-permute-done | bytes 2097184 | tf_op jit(solution)/shard_map/ppermute | solution.py:13
  38.5 44.2 %collective-permute-done.2 = bf16[512,2048]{1,0:T(8,128)(2,1)S(1)} collective-permute-done((bf16[512,2048]{1,0:T(8,128)(2,1)S(1)}, bf16[512,2048]{1,0:T(8,128)(2,1)S(1)}, u32[]{:S(2)}, u32[]{:S(2)}) %collective-permute-start.2) | collective-permute-done | bytes 2097184 | tf_op jit(solution)/shard_map/ppermute | solution.py:13
  86.8 42.0 %collective-permute-done.3 = bf16[512,2048]{1,0:T(8,128)(2,1)} collective-permute-done((bf16[512,2048]{1,0:T(8,128)(2,1)S(1)}, bf16[512,2048]{1,0:T(8,128)(2,1)}, u32[]{:S(2)}, u32[]{:S(2)}) %collective-permute-start.3) | collective-permute-done | bytes 2097184 | tf_op jit(solution)/shard_map/ppermute | solution.py:13
  132.5 43.3 %collective-permute-done.4 = bf16[512,2048]{1,0:T(8,128)(2,1)} collective-permute-done((bf16[512,2048]{1,0:T(8,128)(2,1)}, bf16[512,2048]{1,0:T(8,128)(2,1)}, u32[]{:S(2)}, u32[]{:S(2)}) %collective-permute-start.4) | collective-permute-done | bytes 2097184 | tf_op jit(solution)/shard_map/ppermute | solution.py:13
  213.2 13.8 %fusion.7 = bf16[512,4096]{0,1:T(8,128)(2,1)} fusion(bf16[8192,2048]{1,0:T(8,128)(2,1)} %constant_dynamic-update-slice_fusion, s32[]{:T(128)S(6)} %select_n.32, bf16[1,512,2048]{2,1,0:T(8,128)(2,1)S(1)} %copy-done), kind=kOutput, calls=%fused_computation.7 | convolution fusion | flops 8592031744 | bytes 23068676 | tf_op jit(solution)/shard_map/dot_general | solution.py:79
  227.0 6.4 copy.47
  235.4 51.0 %all-reduce.5 = f32[256]{0:T(256)S(1)} all-reduce(f32[256]{0:T(256)S(1)} %dynamic-update-slice.3), channel_id=1, replica_groups=mesh['dp'=8,'ctx'=4] {'dp','ctx'}, use_global_device_ids=true, to_apply=%add.5 | all-reduce | flops 256 | bytes 2048
  286.4 70.0 %all_gather.9 = f32[256,128]{1,0:T(8,128)S(1)} all-gather(f32[8,128]{1,0:T(8,128)S(1)} %copy-done.25), channel_id=1, replica_groups=mesh['dp'=8,'ctx'=4] {'dp','ctx'}, dimensions={0}, use_global_device_ids=true | all-gather | bytes 135168 | tf_op jit(solution)/shard_map/all_gather | solution.py:56
  359.7 6.6 slice.93
  366.3 19.0 %reshape.175 = bf16[128,255,256]{2,1,0:T(8,128)(2,1)} reshape(bf16[32640,256]{1,0:T(8,128)(2,1)} %slice.93) | data formatting | bytes 33423360 | tf_op jit(solution)/shard_map/reshape | solution.py:34
  385.4 11.9 %broadcast_select_fusion = bf16[128,255,256]{2,1,0:T(8,128)(2,1)} fusion(bf16[128,255,256]{2,1,0:T(8,128)(2,1)} %reshape.175, pred[128,255]{1,0:T(8,128)(4,1)S(1)} %subtract_compare_fusion), kind=kLoop, calls=%fused_computation | loop fusion | flops 8355840 | bytes 33456000 | tf_op jit(solution)/shard_map/jit(_where)/select_n | solution.py:39
  397.3 22.9 %copy.37 = bf16[128,255,256]{1,0,2:T(8,128)(2,1)} copy(bf16[128,255,256]{2,1,0:T(8,128)(2,1)} %broadcast_select_fusion) | data formatting | bytes 33423360 | tf_op jit(solution)/shard_map/jit(_where)/select_n | solution.py:39
  424.0 7.4 convolution_bitcast_fusion.4
  436.7 4.1 slice.94
  448.1 10.0 %collective-permute-done.8 = bf16[127,4096]{1,0:T(8,128)(2,1)} collective-permute-done((bf16[127,4096]{1,0:T(8,128)(2,1)}, bf16[127,4096]{1,0:T(8,128)(2,1)}, u32[]{:S(2)}, u32[]{:S(2)}) %collective-permute-start.8) | collective-permute-done | bytes 1040416 | tf_op jit(solution)/shard_map/ppermute | solution.py:23
  458.1 3.4 convert_add_fusion
  461.5 6.3 scatter-add.4
  467.8 3.9 fusion.28
  474.2 16.5 %collective-permute-done = bf16[127,4096]{1,0:T(8,128)(2,1)S(1)} collective-permute-done((bf16[127,4096]{1,0:T(8,128)(2,1)S(1)}, bf16[127,4096]{1,0:T(8,128)(2,1)S(1)}, u32[]{:S(2)}, u32[]{:S(2)}) %collective-permute-start) | collective-permute-done | bytes 1040416 | tf_op jit(solution)/shard_map/ppermute | solution.py:23
  492.3 4.1 copy.35
  496.3 12.3 %fusion.40 = f32[256,16,128]{2,1,0:T(8,128)} fusion(bf16[255,256,16]{0,2,1:T(8,128)(2,1)} %bitcast.105, bf16[128,255,256]{1,0,2:T(8,128)(2,1)} %copy.37), kind=kOutput, calls=%fused_computation.78 | convolution fusion | flops 267386880 | bytes 20897792 | tf_op jit(solution)/shard_map/tsg,sgc->tgc/dot_general | solution.py:69
  508.6 5.7 convolution_bitcast_fusion.3
  514.3 4.5 convolution_bitcast_fusion.2
  518.9 4.5 convolution_bitcast_fusion.1
  525.4 9.0 copy.42
  534.4 9.5 %reshape.179 = f32[32640,64]{0,1:T(8,128)} reshape(f32[128,255,64]{1,0,2:T(8,128)} %copy.42) | data formatting | bytes 16711680 | tf_op jit(solution)/shard_map/reshape | solution.py:108
  543.9 4.1 concatenate.32
  548.0 5.7 copy.50
  553.7 9.0 copy.43
  562.7 9.3 %reshape.181 = f32[32640,64]{0,1:T(8,128)} reshape(f32[128,255,64]{1,0,2:T(8,128)} %copy.43) | data formatting | bytes 16711680 | tf_op jit(solution)/shard_map/reshape | solution.py:108
  572.0 4.0 concatenate.33
  576.1 5.7 copy.51
  581.8 9.0 copy.44
  590.8 9.8 %reshape.183 = f32[32640,64]{0,1:T(8,128)} reshape(f32[128,255,64]{1,0,2:T(8,128)} %copy.44) | data formatting | bytes 16711680 | tf_op jit(solution)/shard_map/reshape | solution.py:108
  600.5 4.0 concatenate.34
  604.6 5.7 copy.52
  610.4 4.5 convolution_bitcast_fusion
  614.9 9.0 copy.45
  623.9 9.3 %reshape.185 = f32[32640,64]{0,1:T(8,128)} reshape(f32[128,255,64]{1,0,2:T(8,128)} %copy.45) | data formatting | bytes 16711680 | tf_op jit(solution)/shard_map/reshape | solution.py:108
  633.1 4.2 concatenate.35
  637.4 5.7 copy.53
  643.1 6.4 fusion.13
  650.6 14.7 %convolution_convert_fusion = bf16[4096,2048]{1,0:T(8,128)(2,1)} fusion(bf16[512,4096]{0,1:T(8,128)(2,1)} %all-gather.2.cloned.1.call-done, bf16[1,512,2048]{2,1,0:T(8,128)(2,1)S(1)} %copy-done), kind=kOutput, calls=%fused_computation.1 | convolution fusion | flops 8598323200 | bytes 23068672 | tf_op jit(solution)/shard_map/dot_general | solution.py:123
  667.9 44.9 %all-reduce.7 = f32[256]{0:T(256)S(1)} all-reduce(f32[256]{0:T(256)S(1)} %neg.8), channel_id=5, replica_groups=mesh['dp'=8,'ctx'=4] {'dp','ctx'}, use_global_device_ids=true, to_apply=%region_8.9.clone | all-reduce | flops 256 | bytes 2048
  713.4 64.2 %all-reduce.10.cloned.1.call-done = f32[256,128]{1,0:T(8,128)} async-done(((f32[256,128]{1,0:T(8,128)}), f32[256,128]{1,0:T(8,128)}) %all-reduce.10.cloned.1.call-update) | async-done | bytes 131088
  778.9 14.6 %fusion.17 = bf16[1,512,2048]{2,1,0:T(8,128)(2,1)} fusion(bf16[512,4096]{0,1:T(8,128)(2,1)} %all-gather.2.cloned.1.call-done, bf16[8192,2048]{1,0:T(8,128)(2,1)} %constant_dynamic-update-slice_fusion, s32[]{:T(128)S(6)} %select_n.32), kind=kOutput, calls=%fused_computation.21 | convolution fusion | flops 8590983168 | bytes 23068676 | tf_op jit(solution)/shard_map/dot_general | solution.py:75
  793.5 103.0 %reduce-scatter.5.cloned.1.call-done = bf16[512,2048]{1,0:T(8,128)(2,1)} async-done(((bf16[4096,2048]{1,0:T(8,128)(2,1)}), bf16[512,2048]{1,0:T(8,128)(2,1)}) %reduce-scatter.5.cloned.1.call-update) | async-done | bytes 2097168 | tf_op jit(solution)/shard_map/reduce_scatter | solution.py:122
  896.5 4.1 convert_element_type.87
  (129 shorter events, 82.8 us)
Async XLA Ops:
  7.2 206.0 %copy-start = (bf16[1,512,2048]{2,1,0:T(8,128)(2,1)S(1)}, bf16[1,512,2048]{2,1,0:T(8,128)(2,1)}, u32[]{:S(2)}) copy-start(bf16[1,512,2048]{2,1,0:T(8,128)(2,1)} %param.17) | copy-start | bytes 6291460
  7.2 413.1 %reduce-scatter.7.cloned.1.call-start = ((), (), s32[]{:S(2)}) async-start(), calls=%async_computation.4 | async-start | bytes 5242880
  7.2 27.3 %collective-permute-start.1 = (bf16[512,2048]{1,0:T(8,128)(2,1)}, bf16[512,2048]{1,0:T(8,128)(2,1)S(1)}, u32[]{:S(2)}, u32[]{:S(2)}) collective-permute-start(bf16[512,2048]{1,0:T(8,128)(2,1)} %param.16), channel_id=1, source_target_pairs={{0,4},{4,8},{8,12},{12,16},{16,20},{20,24},{24,28},{28,0},{1,5},{5... | collective-permute-start | bytes 6291464 | tf_op jit(solution)/shard_map/ppermute | solution.py:13
  34.5 1.3 copy-start.10
  35.9 46.9 %collective-permute-start.2 = (bf16[512,2048]{1,0:T(8,128)(2,1)S(1)}, bf16[512,2048]{1,0:T(8,128)(2,1)S(1)}, u32[]{:S(2)}, u32[]{:S(2)}) collective-permute-start(bf16[512,2048]{1,0:T(8,128)(2,1)S(1)} %collective-permute-done.1), channel_id=1, source_target_pairs={{0,4},{4,8},{8,12},{12,16},{16,20},{20,24},{24,28},{28,0},{1,5},{5... | collective-permute-start | bytes 6291464 | tf_op jit(solution)/shard_map/ppermute | solution.py:13
  35.9 46.9 %collective-permute-start.5 = (bf16[512,2048]{1,0:T(8,128)(2,1)}, bf16[512,2048]{1,0:T(8,128)(2,1)S(1)}, u32[]{:S(2)}, u32[]{:S(2)}) collective-permute-start(bf16[512,2048]{1,0:T(8,128)(2,1)} %param.16), channel_id=1, source_target_pairs={{0,28},{4,0},{8,4},{12,8},{16,12},{20,16},{24,20},{28,24},{1,29},{... | collective-permute-start | bytes 6291464 | tf_op jit(solution)/shard_map/ppermute | solution.py:15
  82.7 46.8 %copy-start.14 = (bf16[512,2048]{1,0:T(8,128)(2,1)}, bf16[512,2048]{1,0:T(8,128)(2,1)S(1)}, u32[]{:S(2)}) copy-start(bf16[512,2048]{1,0:T(8,128)(2,1)S(1)} %collective-permute-done.2) | copy-start | bytes 6291460
  82.7 46.1 %collective-permute-start.3 = (bf16[512,2048]{1,0:T(8,128)(2,1)S(1)}, bf16[512,2048]{1,0:T(8,128)(2,1)}, u32[]{:S(2)}, u32[]{:S(2)}) collective-permute-start(bf16[512,2048]{1,0:T(8,128)(2,1)S(1)} %collective-permute-done.2), channel_id=1, source_target_pairs={{0,4},{4,8},{8,12},{12,16},{16,20},{20,24},{24,28},{28,0},{1,5},{5... | collective-permute-start | bytes 6291464 | tf_op jit(solution)/shard_map/ppermute | solution.py:13
  82.8 1.4 copy-start.12
  84.2 45.4 %collective-permute-start.6 = (bf16[512,2048]{1,0:T(8,128)(2,1)S(1)}, bf16[512,2048]{1,0:T(8,128)(2,1)}, u32[]{:S(2)}, u32[]{:S(2)}) collective-permute-start(bf16[512,2048]{1,0:T(8,128)(2,1)S(1)} %collective-permute-done.5), channel_id=1, source_target_pairs={{0,28},{4,0},{8,4},{12,8},{16,12},{20,16},{24,20},{28,24},{1,29},{... | collective-permute-start | bytes 6291464 | tf_op jit(solution)/shard_map/ppermute | solution.py:15
  128.9 46.9 %collective-permute-start.4 = (bf16[512,2048]{1,0:T(8,128)(2,1)}, bf16[512,2048]{1,0:T(8,128)(2,1)}, u32[]{:S(2)}, u32[]{:S(2)}) collective-permute-start(bf16[512,2048]{1,0:T(8,128)(2,1)} %collective-permute-done.3), channel_id=1, source_target_pairs={{0,4},{4,8},{8,12},{12,16},{16,20},{20,24},{24,28},{28,0},{1,5},{5... | collective-permute-start | bytes 6291464 | tf_op jit(solution)/shard_map/ppermute | solution.py:13
  129.5 61.8 %collective-permute-start.7 = (bf16[512,2048]{1,0:T(8,128)(2,1)}, bf16[512,2048]{1,0:T(8,128)(2,1)}, u32[]{:S(2)}, u32[]{:S(2)}) collective-permute-start(bf16[512,2048]{1,0:T(8,128)(2,1)} %collective-permute-done.6), channel_id=1, source_target_pairs={{0,28},{4,0},{8,4},{12,8},{16,12},{20,16},{24,20},{28,24},{1,29},{... | collective-permute-start | bytes 6291464 | tf_op jit(solution)/shard_map/ppermute | solution.py:15
  132.5 49.8 %copy-start.15 = (bf16[512,2048]{1,0:T(8,128)(2,1)S(1)}, bf16[512,2048]{1,0:T(8,128)(2,1)}, u32[]{:S(2)}) copy-start(bf16[512,2048]{1,0:T(8,128)(2,1)} %copy-done.14) | copy-start | bytes 6291460
  178.9 4.8 copy-start.11
  182.2 3.0 copy-start.9
  183.7 3.1 copy-start.13
  233.4 1.7 copy-start.27
  233.4 53.0 %copy-start.25 = (f32[8,128]{1,0:T(8,128)S(1)}, f32[8,128]{1,0:T(8,128)}, u32[]{:S(2)}) copy-start(f32[8,128]{1,0:T(8,128)} %param.14) | copy-start | bytes 12292
  233.5 417.2 %all-gather.2.cloned.1.call-start = ((), (), s32[]{:S(2)}) async-start(), calls=%async_computation.2 | async-start | bytes 5242880 | tf_op jit(solution)/shard_map/all_gather | solution.py:74
  235.1 187.4 %copy-start.3 = (bf16[1,128,4096]{1,2,0:T(8,128)(2,1)}, bf16[1,128,4096]{1,2,0:T(8,128)(2,1)S(1)}, u32[]{:S(2)}) copy-start(bf16[1,128,4096]{1,2,0:T(8,128)(2,1)S(1)} %copy.34) | copy-start | bytes 3145732
  286.4 70.0 %copy-start.23 = (f32[256]{0:T(256)}, f32[256]{0:T(256)S(1)}, u32[]{:S(2)}) copy-start(f32[256]{0:T(256)S(1)} %neg.7) | copy-start | bytes 3076
  356.4 0.7 copy-start.19
  366.3 19.0 %copy-start.26 = (s32[1,128]{1,0:T(1,128)S(1)}, s32[1,128]{1,0:T(1,128)}, u32[]{:S(2)}) copy-start(s32[1,128]{1,0:T(1,128)} %param.13) | copy-start | bytes 1540
  424.0 7.4 copy-start.16
  431.4 2.0 copy-start.1
  435.1 5.7 copy-start.2
  435.1 23.0 %collective-permute-start.8 = (bf16[127,4096]{1,0:T(8,128)(2,1)}, bf16[127,4096]{1,0:T(8,128)(2,1)}, u32[]{:S(2)}, u32[]{:S(2)}) collective-permute-start(bf16[127,4096]{1,0:T(8,128)(2,1)} %copy.39), channel_id=1, source_target_pairs={{1,0},{2,1},{3,2},{5,4},{6,5},{7,6},{9,8},{10,9},{11,10},{13,12},{... | collective-permute-start | bytes 3121160 | tf_op jit(solution)/shard_map/ppermute | solution.py:23
  448.1 19.7 %copy-start.21 = (bf16[1,128,4096]{2,1,0:T(8,128)(2,1)S(1)}, bf16[1,128,4096]{2,1,0:T(8,128)(2,1)}, u32[]{:S(2)}) copy-start(bf16[1,128,4096]{2,1,0:T(8,128)(2,1)} %param.11) | copy-start | bytes 3145732
  472.0 18.7 %collective-permute-start = (bf16[127,4096]{1,0:T(8,128)(2,1)S(1)}, bf16[127,4096]{1,0:T(8,128)(2,1)S(1)}, u32[]{:S(2)}, u32[]{:S(2)}) collective-permute-start(bf16[127,4096]{1,0:T(8,128)(2,1)S(1)} %slice.92), channel_id=1, source_target_pairs={{0,1},{1,2},{2,3},{4,5},{5,6},{6,7},{8,9},{9,10},{10,11},{12,13},{... | collective-permute-start | bytes 3121160 | tf_op jit(solution)/shard_map/ppermute | solution.py:23
  496.3 12.3 %copy-start.17 = (bf16[128,4096]{0,1:T(8,128)(2,1)S(1)}, bf16[128,4096]{0,1:T(8,128)(2,1)}, u32[]{:S(2)}) copy-start(bf16[128,4096]{0,1:T(8,128)(2,1)} %copy-done.16) | copy-start | bytes 3145732
  508.6 5.7 copy-start.7
  518.9 4.6 copy-start.4
  518.9 4.6 copy-start.5
  518.9 4.6 copy-start.6
  525.2 252.5 %all-reduce.10.cloned.1.call-start = ((), (), s32[]{:S(2)}) async-start(), calls=%async_computation.5 | async-start | bytes 262144
  604.6 5.8 copy-start.8
  633.1 9.9 %slice-start = ((s8[8388608]{0:T(1024)(128)(4,1)}), s8[4194304]{0:T(1024)(128)(4,1)S(1)}, s32[]{:S(2)}) async-start(s8[8388608]{0:T(1024)(128)(4,1)} %bitcast.99), calls=%async_computation.6 | async-start | bytes 8388608
  637.3 5.7 slice-start.1
  637.3 5.7 copy-start.22
  643.1 6.7 copy-start.20
  643.1 6.7 copy-start.24
  650.6 246.0 %reduce-scatter.5.cloned.1.call-start = ((), (), s32[]{:S(2)}) async-start(), calls=%async_computation.3 | async-start | bytes 18874368 | tf_op jit(solution)/shard_map/reduce_scatter | solution.py:122
  665.4 1.2 copy-start.18
Sparse Core Ops, SparseCore 0:
  233.6 86.0 reduce-scatter.6
  525.3 85.2 all-gather.1
  650.7 126.9 all-reduce.9
  781.5 114.9 reduce-scatter.4
